TPU v7x, 256 devices: a whole 4x4x8 slice. The times are simulated.
256 devices in a mesh: grp: 2 (over core), row: 4 (over y), col: 32 (over z, x).
Axes of the slice: x: 4, y: 4, z: 8, core: 2. Of those that a mesh axis runs over, the one named last changes fastest.
Arguments:
- sub_rhs: float32 [2, 3, 4, 32, 256, 512], P('grp', None, 'row', 'col'), may hold values from -6 to 6
- sub_dinv: float32 [2, 3, 4, 32, 256, 256], P('grp', None, 'row', 'col')
- anc_rhs: float32 [4, 32, 256, 512], P('row', 'col'), may hold values from -6 to 6
- anc_dinv: float32 [4, 32, 256, 256], P('row', 'col')
- tiles: bfloat16 [2, 4, 32, 3, 16, 256, 256], P('grp', 'row', 'col'), may hold values from -0.09375 to 0.09375
- tile_target: int32 [2, 4, 32, 3, 16], P('grp', 'row', 'col'), may hold values from 0 to 11, as said below
- tile_source: int32 [2, 4, 32, 3, 16], P('grp', 'row', 'col'), may hold values from 0 to 31, as said below
- tile_count: int32 [2, 4, 32, 3], P('grp', 'row', 'col'), may hold values from 1 to 16, as said below
Outputs:
- sub_solution: float32 [2, 3, 4, 32, 256, 512], P('grp', None, 'row', 'col')
- anc_solution: float32 [4, 32, 256, 512], P('row', 'col')
Inputs may be any that keep to these rules, and one draw needn't show every extreme that they name: `tile_target`: entry [g, q, c, k, j] is (t - 1) * 4 + r for a target level t with k < t <= 3 (t = 3 is the ancestor level) and a process row r; entries at slots j >= tile_count are unused. `tile_source`: Non-decreasing along the last dimension. `tile_count`: for every source level some device holds exactly 16 live tiles.
All inputs are finite; a program needn't handle non-finite values.
Results may differ from a plain program's by a relative error of at most 0.0027.
Values may be sent and summed in bfloat16 or wider, within the bound.
No kernel may reach another device: no remote copies, remote signals or barrier semaphores. Data moves between devices by JAX's collectives and lax.ppermute only.
A program may use at most 128 MiB of HBM per device.

v0:
```python
import jax
import jax.numpy as jnp
from jax import lax
from jax.sharding import PartitionSpec as P


def split_up(shard, dim, peers):
    lengths = shard.shape
    pieces = shard.reshape(*lengths[:dim], peers, lengths[dim] // peers, *lengths[dim + 1 :])
    return jnp.moveaxis(pieces, dim, 0)


def sum_at_owner(shard, axis, dim):
    peers = lax.axis_size(axis)
    pieces = lax.all_to_all(split_up(shard, dim, peers), axis, 0, 0, tiled=True)
    return jnp.sum(pieces, axis=0)


def from_everyone(shard, axis):
    copies = jnp.broadcast_to(shard, (lax.axis_size(axis), *shard.shape))
    return lax.all_to_all(copies, axis, split_axis=0, concat_axis=0, tiled=True)


def of_everyone(shard, axis):
    return from_everyone(shard, axis).sum(axis=0)


def spread_terms(pending, gathered, blocks, targets, sources, live_count):
    slots = blocks.shape[0]
    fetched = jnp.take(gathered, sources, axis=0)
    products = jnp.einsum("tij,tjw->tiw", blocks, fetched, preferred_element_type=jnp.float32)
    live = jnp.arange(slots, dtype=jnp.int32) < live_count
    codes = jnp.arange(pending.shape[0], dtype=jnp.int32)
    selector = ((targets[:, None] == codes[None, :]) & live[:, None]).astype(jnp.float32)
    return pending + jnp.einsum("tk,tiw->kiw", selector, products, precision=lax.Precision.HIGHEST)


def on_device(sub_rhs, sub_dinv, anc_rhs, anc_dinv, tiles, tile_target, tile_source, tile_count):
    highest = lax.Precision.HIGHEST
    rhs_levels = sub_rhs[0, :, 0, 0]
    inverses = sub_dinv[0, :, 0, 0]
    blocks = tiles[0, 0, 0]
    targets = tile_target[0, 0, 0]
    sources = tile_source[0, 0, 0]
    counts = tile_count[0, 0, 0]
    depth, block_rows, columns = rhs_levels.shape
    row_count = lax.axis_size("row")
    pending = jnp.zeros((depth * row_count, block_rows, columns), jnp.float32)
    solved = []
    for source_level in range(depth):
        remainder = rhs_levels[source_level]
        if source_level > 0:
            arrived = sum_at_owner(
                pending[(source_level - 1) * row_count : source_level * row_count], "row", 0
            )
            remainder = remainder - arrived[0]
        current = jnp.dot(
            inverses[source_level], remainder, precision=highest, preferred_element_type=jnp.float32
        )
        solved.append(current)
        rounded = current.astype(jnp.bfloat16)[None]
        everyone = lax.all_gather(rounded, "col", axis=0, tiled=True)
        pending = spread_terms(
            pending,
            everyone,
            blocks[source_level],
            targets[source_level],
            sources[source_level],
            counts[source_level],
        )
    ancestor_part = pending[(depth - 1) * row_count :]
    ancestor_rhs = anc_rhs[0, 0]
    ancestor_inverse = anc_dinv[0, 0]
    group_part = sum_at_owner(ancestor_part, "row", 0)[0]
    combined = of_everyone(group_part, "grp")
    ancestor = jnp.dot(
        ancestor_inverse,
        ancestor_rhs - combined,
        precision=highest,
        preferred_element_type=jnp.float32,
    )
    sub_out = jnp.stack(solved)[None, :, None, None]
    return (sub_out, ancestor[None, None])


def solution(mesh):
    placed = (
        P("grp", None, "row", "col", None, None),
        P("grp", None, "row", "col", None, None),
        P("row", "col", None, None),
        P("row", "col", None, None),
        P("grp", "row", "col", None, None, None, None),
        P("grp", "row", "col", None, None),
        P("grp", "row", "col", None, None),
        P("grp", "row", "col", None),
    )
    return jax.shard_map(
        on_device,
        mesh=mesh,
        in_specs=placed,
        out_specs=(P("grp", None, "row", "col", None, None), P("row", "col", None, None)),
        check_vma=False,
    )
```

profile of v0, /device:TPU:1, one launch (start us, length us, event | category | flops | bytes accessed | tf_op | source)
XLA Modules:
  0.0 535.7 jit_solution(11485842534469327376)
XLA Ops:
  7.2 0.0 all-gather.7.cloned.1.call-start
  7.2 2.5 fusion.66
  9.7 0.0 all-gather.9.cloned.1.call-start
  9.8 1.4 fusion.65
  11.2 0.6 iota_compare_fusion.5
  11.8 0.7 compare_and_fusion
  12.6 0.7 slice_bitcast_fusion.2
  13.2 99.7 %all-gather.7.cloned.1.call-done = bf16[8192,512]{1,0:T(8,128)(2,1)} async-done(((bf16[256,512]{1,0:T(8,128)(2,1)}), bf16[8192,512]{1,0:T(8,128)(2,1)}) %all-gather.7.cloned.1.call-update) | async-done | bytes 8388624 | tf_op jit(solution)/shard_map/all_gather | solution.py:62
  112.9 6.2 %gather_fusion = bf16[16,256,512]{2,1,0:T(8,128)(2,1)} fusion(bf16[32,256,512]{2,1,0:T(8,128)(2,1)} %bitcast.126, s32[1024]{0:T(1024)S(1)} %pad_clamp_fusion.2), kind=kCustom, calls=%fused_computation.clone | custom fusion | bytes 8388672 | tf_op jit(solution)/shard_map/jit(_take)/gather | solution.py:30
  119.1 7.6 %fusion.9 = f32[16,256,512]{1,2,0:T(8,128)} fusion(bf16[16,256,512]{2,1,0:T(8,128)(2,1)} %gather_fusion, pred[16]{0:T(512)(128)(4,1)S(1)} %get-tuple-element.20, bf16[1,1,1,3,16,256,256]{6,5,4,3,2,1,0:T(8,128)(2,1)} %param.14), kind=kOutput, calls=%fused_computation.13 | convolution fusion | flops 1075838976 | bytes 14680080 | tf_op jit(solution)/shard_map/tij,tjw->tiw/dot_general | solution.py:31
  126.7 10.5 %copy.32 = f32[16,256,512]{2,0,1:T(8,128)} copy(f32[16,256,512]{1,2,0:T(8,128)} %fusion.9) | data formatting | bytes 16777216 | tf_op jit(solution)/shard_map/tij,tjw->tiw/dot_general | solution.py:31
  137.2 12.8 %fusion.47 = f32[12,256,512]{2,0,1:T(8,128)S(1)} fusion(f32[16,256,512]{2,0,1:T(8,128)} %copy.32, s32[16]{0:T(128)S(1)} %get-tuple-element.18, pred[16]{0:T(512)(128)(4,1)S(1)} %iota_compare_fusion.5), kind=kOutput, calls=%fused_computation.58 | convolution fusion | flops 301990272 | bytes 14680144 | tf_op jit(solution)/shard_map/tk,tiw->kiw/dot_general | solution.py:35
  149.9 3.2 copy-done.1
  153.2 0.5 slice_bitcast_fusion.1
  153.7 0.7 copy.33
  154.4 28.5 %all_to_all.20 = f32[4,1,256,512]{3,2,1,0:T(8,128)S(1)} all-to-all(f32[4,1,256,512]{3,2,1,0:T(8,128)S(1)} %copy.33), channel_id=1, replica_groups=mesh['grp'=2,'row'=4,'col'=32] {'row'}, dimensions={0} | all-to-all | bytes 4194304 | tf_op jit(solution)/shard_map/all_to_all | solution.py:15
  182.9 1.0 reduce_sum.38
  183.9 2.6 bitcast_convert_fusion.1
  186.6 0.2 all-gather.11.cloned.1.call-start
  186.8 0.6 iota_compare_fusion.4
  187.4 94.4 %all-gather.9.cloned.1.call-done = bf16[8192,512]{1,0:T(8,128)(2,1)} async-done(((bf16[256,512]{1,0:T(8,128)(2,1)}), bf16[8192,512]{1,0:T(8,128)(2,1)}) %all-gather.9.cloned.1.call-update) | async-done | bytes 8388624 | tf_op jit(solution)/shard_map/all_gather | solution.py:62
  281.8 6.1 %gather_fusion.1 = bf16[16,256,512]{2,1,0:T(8,128)(2,1)} fusion(bf16[32,256,512]{2,1,0:T(8,128)(2,1)} %bitcast.127, s32[1024]{0:T(1024)S(1)} %pad_clamp_fusion.1), kind=kCustom, calls=%fused_computation.1.clone | custom fusion | bytes 8388672 | tf_op jit(solution)/shard_map/jit(_take)/gather | solution.py:30
  287.9 7.6 %fusion.12 = f32[16,256,512]{1,2,0:T(8,128)} fusion(bf16[16,256,512]{2,1,0:T(8,128)(2,1)} %gather_fusion.1, pred[16]{0:T(512)(128)(4,1)S(1)} %get-tuple-element.22, bf16[1,1,1,3,16,256,256]{6,5,4,3,2,1,0:T(8,128)(2,1)} %param.14), kind=kOutput, calls=%fused_computation.14 | convolution fusion | flops 1075838976 | bytes 14680080 | tf_op jit(solution)/shard_map/tij,tjw->tiw/dot_general | solution.py:31
  295.5 10.5 %copy.36 = f32[16,256,512]{2,0,1:T(8,128)} copy(f32[16,256,512]{1,2,0:T(8,128)} %fusion.12) | data formatting | bytes 16777216 | tf_op jit(solution)/shard_map/tij,tjw->tiw/dot_general | solution.py:31
  306.0 10.9 %convolution_add_fusion = f32[12,256,512]{2,0,1:T(8,128)S(1)} fusion(f32[12,256,512]{2,0,1:T(8,128)} %copy-done.1, f32[16,256,512]{2,0,1:T(8,128)} %copy.36, s32[16]{0:T(128)S(1)} %get-tuple-element.19, pred[16]{0:T(512)(128)(4,1)S(1)} %iota_compare_fusion.4), kind=kOutput, calls=%fused_computation.12 | convolution fusion | flops 303563136 | bytes 20971600 | tf_op jit(solution)/shard_map/tk,tiw->kiw/dot_general | solution.py:35
  316.9 3.2 copy-done.2
  320.1 0.6 slice_bitcast_fusion
  320.7 0.7 copy.37
  321.4 28.5 %all_to_all.21 = f32[4,1,256,512]{3,2,1,0:T(8,128)S(1)} all-to-all(f32[4,1,256,512]{3,2,1,0:T(8,128)S(1)} %copy.37), channel_id=1, replica_groups=mesh['grp'=2,'row'=4,'col'=32] {'row'}, dimensions={0} | all-to-all | bytes 4194304 | tf_op jit(solution)/shard_map/all_to_all | solution.py:15
  349.9 1.0 reduce_sum.39
  350.9 2.8 bitcast_convert_fusion
  353.7 0.6 iota_compare_fusion.3
  354.4 94.6 %all-gather.11.cloned.1.call-done = bf16[8192,512]{1,0:T(8,128)(2,1)} async-done(((bf16[256,512]{1,0:T(8,128)(2,1)}), bf16[8192,512]{1,0:T(8,128)(2,1)}) %all-gather.11.cloned.1.call-update) | async-done | bytes 8388624 | tf_op jit(solution)/shard_map/all_gather | solution.py:62
  449.0 6.1 %gather_fusion.2 = bf16[16,256,512]{2,1,0:T(8,128)(2,1)} fusion(bf16[32,256,512]{2,1,0:T(8,128)(2,1)} %bitcast.128, s32[1024]{0:T(1024)S(1)} %pad_clamp_fusion), kind=kCustom, calls=%fused_computation.2.clone | custom fusion | bytes 8388672 | tf_op jit(solution)/shard_map/jit(_take)/gather | solution.py:30
  455.1 7.6 %fusion.15 = f32[16,256,512]{1,2,0:T(8,128)} fusion(bf16[16,256,512]{2,1,0:T(8,128)(2,1)} %gather_fusion.2, pred[16]{0:T(512)(128)(4,1)S(1)} %get-tuple-element.11, bf16[1,1,1,3,16,256,256]{6,5,4,3,2,1,0:T(8,128)(2,1)} %param.14), kind=kOutput, calls=%fused_computation.15 | convolution fusion | flops 1075838976 | bytes 14680080 | tf_op jit(solution)/shard_map/tij,tjw->tiw/dot_general | solution.py:31
  462.7 10.5 %copy.40 = f32[16,256,512]{2,0,1:T(8,128)} copy(f32[16,256,512]{1,2,0:T(8,128)} %fusion.15) | data formatting | bytes 16777216 | tf_op jit(solution)/shard_map/tij,tjw->tiw/dot_general | solution.py:31
  473.2 12.8 %fusion.54 = f32[12,256,512]{2,0,1:T(8,128)S(1)} fusion(f32[16,256,512]{2,0,1:T(8,128)} %copy.40, s32[16]{0:T(128)S(1)} %get-tuple-element.17, pred[16]{0:T(512)(128)(4,1)S(1)} %iota_compare_fusion.3), kind=kOutput, calls=%fused_computation.63 | convolution fusion | flops 301990272 | bytes 14680144 | tf_op jit(solution)/shard_map/tk,tiw->kiw/dot_general | solution.py:35
  485.9 3.2 fusion.18
  489.2 2.0 copy.41
  491.1 4.0 all-to-all-start.2
  495.1 2.3 maximum_bitcast_fusion
  497.4 22.7 %all-to-all-done.2 = f32[4,1,256,512]{3,2,1,0:T(8,128)S(1)} async-done(((f32[4,1,256,512]{3,2,1,0:T(8,128)}), f32[4,1,256,512]{3,2,1,0:T(8,128)S(1)}, u32[]{:S(2)}, u32[]{:S(2)}) %all-to-all-start.2) | async-done | bytes 2097184 | tf_op jit(solution)/shard_map/all_to_all | solution.py:15
  520.1 0.2 reduce_sum.40
  520.4 0.1 broadcast_in_dim.37
  520.5 6.5 %all_to_all.22 = f32[2,256,512]{2,1,0:T(8,128)S(1)} all-to-all(f32[2,256,512]{2,1,0:T(8,128)S(1)} %broadcast_in_dim.37), channel_id=1, replica_groups=mesh['grp'=2,'row'=4,'col'=32] {'grp'}, dimensions={0} | all-to-all | bytes 2097152 | tf_op jit(solution)/shard_map/all_to_all | solution.py:21
  527.0 0.1 reduce_sum.41
  527.1 1.0 convolution_bitcast_fusion
  528.1 1.0 copy.43
  (12 shorter events, 0.1 us)
Async XLA Ops:
  7.2 519.9 %copy-start = (f32[1,1,256,256]{3,2,1,0:T(8,128)S(1)}, f32[1,1,256,256]{3,2,1,0:T(8,128)}, u32[]{:S(2)}) copy-start(f32[1,1,256,256]{3,2,1,0:T(8,128)} %param.13) | copy-start | bytes 786436
  7.2 105.7 %all-gather.7.cloned.1.call-start = ((), (), s32[]{:S(2)}) async-start(), calls=%async_computation.4 | async-start | bytes 8650752 | tf_op jit(solution)/shard_map/all_gather | solution.py:62
  9.7 272.1 %all-gather.9.cloned.1.call-start = ((), (), s32[]{:S(2)}) async-start(), calls=%async_computation.5 | async-start | bytes 8650752 | tf_op jit(solution)/shard_map/all_gather | solution.py:62
  149.9 3.2 copy-start.1
  186.6 262.4 %all-gather.11.cloned.1.call-start = ((), (), s32[]{:S(2)}) async-start(), calls=%async_computation.6 | async-start | bytes 8650752 | tf_op jit(solution)/shard_map/all_gather | solution.py:62
  316.9 3.2 copy-start.2
  491.1 29.0 %all-to-all-start.2 = ((f32[4,1,256,512]{3,2,1,0:T(8,128)}), f32[4,1,256,512]{3,2,1,0:T(8,128)S(1)}, u32[]{:S(2)}, u32[]{:S(2)}) async-start(f32[4,1,256,512]{3,2,1,0:T(8,128)} %copy.41), calls=%async_computation.2 | async-start | bytes 4194304 | tf_op jit(solution)/shard_map/all_to_all | solution.py:15
  497.4 29.7 %copy-start.3 = (f32[1,1,256,512]{3,2,1,0:T(8,128)S(1)}, f32[1,1,256,512]{3,2,1,0:T(8,128)}, u32[]{:S(2)}) copy-start(f32[1,1,256,512]{3,2,1,0:T(8,128)} %param.12) | copy-start | bytes 1572868
Sparse Core Ops, SparseCore 0:
  11.2 101.6 all-gather.6
  186.7 95.0 all-gather.8
  353.8 95.0 all-gather.10
where the time goes:
time: 537 us; the launch traced here: 536 us
  waiting for transfers between devices  311 us (58%)
  matrix products  68.1 us (13%)
  local copies, waits for them, and re-layouts  64 us (12%)
  blocking collectives  63.5 us (12%)
  between operations  13.9 us (3%)
  other arithmetic  10.6 us (2%)
    all_gather x3, waiting for transfers between devices, on_device(): everyone = lax.all_gather(rounded, 'col', axis=0, tiled=True)  289 us
    all_to_all x2, blocking collectives, sum_at_owner(): pieces = lax.all_to_all(split_up(shard, dim, peers), axis, 0, 0, tiled=True)  57 us
    dot_general x3, matrix products, spread_terms(): jnp.einsum('tk,tiw->kiw', selector, products, precision=lax.Precision.HIG...  36.4 us
    dot_general x3, local copies, waits for them, and re-layouts, spread_terms(): jnp.einsum('tij,tjw->tiw', blocks, fetched, preferred_element_type=jnp.fl...  31.4 us
    dot_general x3, matrix products, spread_terms(): jnp.einsum('tij,tjw->tiw', blocks, fetched, preferred_element_type=jnp.fl...  22.8 us
    all_to_all x1, waiting for transfers between devices, sum_at_owner(): pieces = lax.all_to_all(split_up(shard, dim, peers), axis, 0, 0, tiled=True)  22.7 us
    gather x3, local copies, waits for them, and re-layouts, spread_terms(): fetched = jnp.take(gathered, sources, axis=0)  18.4 us
  transfers between devices with their start and end apart: 4, of which 4 were waited for; matrix products, arithmetic and copies ran while one was open for 1% of the time, Pallas kernels for 0%

commit v1 on v0

--- a/solution.py
+++ b/solution.py
@@ -59,7 +59,8 @@
         )
         solved.append(current)
         rounded = current.astype(jnp.bfloat16)[None]
-        everyone = lax.all_gather(rounded, "col", axis=0, tiled=True)
+        sent = jnp.stack([rounded] * lax.axis_size("col"))
+        everyone = jnp.concatenate(lax.all_to_all(sent, "col", 0, 0), axis=0)
         pending = spread_terms(
             pending,
             everyone,

time: 537 us -> 831 us (1.55)
  waiting for transfers between devices: 311 us -> 566 us
  starting transfers between devices: 4.31 us -> 47 us
  between operations: 13.9 us -> 0.88 us
  local copies, waits for them, and re-layouts: 64 us -> 75 us
    all_to_all x0 -> x3, waiting for transfers between devices: none -> 546 us  [on_device(): everyone = jnp.concatenate(lax.all_to_all(sent, 'col', 0, 0), axis=0)]
    all_gather x3 -> x0, waiting for transfers between devices: 289 us -> none  [on_device(): everyone = lax.all_gather(rounded, 'col', axis=0, tiled=True)]
    all_to_all x0 -> x3, starting transfers between devices: none -> 43.4 us  [on_device(): everyone = jnp.concatenate(lax.all_to_all(sent, 'col', 0, 0), axis=0)]
    another operation x0 -> x3, local copies, waits for them, and re-layouts: none -> 12.5 us  [on_device(): sent = jnp.stack([rounded] * lax.axis_size('col'))]
where the time goes in v1:
time: 831 us; the launch traced here: 827 us
  waiting for transfers between devices  566 us (68%)
  local copies, waits for them, and re-layouts  75 us (9%)
  matrix products  66.7 us (8%)
  blocking collectives  61.8 us (7%)
  starting transfers between devices  47 us (6%)
  other arithmetic  9.88 us (1%)
    all_to_all x3, waiting for transfers between devices, on_device(): everyone = jnp.concatenate(lax.all_to_all(sent, 'col', 0, 0), axis=0)  546 us
    all_to_all x2, blocking collectives, sum_at_owner(): pieces = lax.all_to_all(split_up(shard, dim, peers), axis, 0, 0, tiled=True)  53 us
    all_to_all x3, starting transfers between devices, on_device(): everyone = jnp.concatenate(lax.all_to_all(sent, 'col', 0, 0), axis=0)  43.4 us
    dot_general x3, matrix products, spread_terms(): jnp.einsum('tk,tiw->kiw', selector, products, precision=lax.Precision.HIG...  36.4 us
    dot_general x3, local copies, waits for them, and re-layouts, spread_terms(): jnp.einsum('tij,tjw->tiw', blocks, fetched, preferred_element_type=jnp.fl...  31.4 us
    dot_general x3, matrix products, spread_terms(): jnp.einsum('tij,tjw->tiw', blocks, fetched, preferred_element_type=jnp.fl...  22.8 us
    all_to_all x1, waiting for transfers between devices, sum_at_owner(): pieces = lax.all_to_all(split_up(shard, dim, peers), axis, 0, 0, tiled=True)  20.4 us
    gather x3, local copies, waits for them, and re-layouts, spread_terms(): fetched = jnp.take(gathered, sources, axis=0)  18.4 us
  transfers between devices with their start and end apart: 4, of which 4 were waited for; matrix products, arithmetic and copies ran while one was open for 1% of the time, Pallas kernels for 0%

profile of v1, /device:TPU:1, one launch (start us, length us, event | category | flops | bytes accessed | tf_op | source)
XLA Modules:
  0.0 827.3 jit_solution(10006433004342860348)
XLA Ops:
  0.6 1.8 fusion.66
  2.4 4.2 stack.22
  6.6 12.1 %all-to-all-start = ((bf16[32,1,256,512]{3,2,1,0:T(8,128)(2,1)}), bf16[32,1,256,512]{3,2,1,0:T(8,128)(2,1)}, u32[]{:S(2)}, u32[]{:S(2)}) async-start(bf16[32,1,256,512]{3,2,1,0:T(8,128)(2,1)} %stack.22), calls=%async_computation | async-start | bytes 16777216 | tf_op jit(solution)/shard_map/all_to_all | solution.py:63
  18.8 0.6 fusion.65
  19.4 0.6 iota_compare_fusion.5
  20.1 186.2 %all-to-all-done = bf16[32,1,256,512]{3,2,1,0:T(8,128)(2,1)} async-done(((bf16[32,1,256,512]{3,2,1,0:T(8,128)(2,1)}), bf16[32,1,256,512]{3,2,1,0:T(8,128)(2,1)}, u32[]{:S(2)}, u32[]{:S(2)}) %all-to-all-start) | async-done | bytes 8388640 | tf_op jit(solution)/shard_map/all_to_all | solution.py:63
  206.3 6.2 gather_fusion
  212.5 7.6 fusion.9
  220.1 10.5 %copy.45 = f32[16,256,512]{2,0,1:T(8,128)} copy(f32[16,256,512]{1,2,0:T(8,128)} %fusion.9) | data formatting | bytes 16777216 | tf_op jit(solution)/shard_map/tij,tjw->tiw/dot_general | solution.py:31
  230.5 12.8 %fusion.47 = f32[12,256,512]{2,0,1:T(8,128)S(1)} fusion(f32[16,256,512]{2,0,1:T(8,128)} %copy.45, s32[16]{0:T(128)S(1)} %get-tuple-element.20, pred[16]{0:T(512)(128)(4,1)S(1)} %iota_compare_fusion.5), kind=kOutput, calls=%fused_computation.58 | convolution fusion | flops 301990272 | bytes 14680144 | tf_op jit(solution)/shard_map/tk,tiw->kiw/dot_general | solution.py:35
  243.3 3.2 copy-done.1
  246.6 0.5 slice_bitcast_fusion.1
  247.1 0.7 copy.46
  247.7 28.0 %all_to_all.35 = f32[4,1,256,512]{3,2,1,0:T(8,128)S(1)} all-to-all(f32[4,1,256,512]{3,2,1,0:T(8,128)S(1)} %copy.46), channel_id=1, replica_groups=mesh['grp'=2,'row'=4,'col'=32] {'row'}, dimensions={0} | all-to-all | bytes 4194304 | tf_op jit(solution)/shard_map/all_to_all | solution.py:15
  275.7 1.0 reduce_sum.38
  276.8 1.9 bitcast_convert_fusion.1
  278.7 4.2 stack.24
  282.9 16.8 %all-to-all-start.2 = ((bf16[32,1,256,512]{3,2,1,0:T(8,128)(2,1)}), bf16[32,1,256,512]{3,2,1,0:T(8,128)(2,1)}, u32[]{:S(2)}, u32[]{:S(2)}) async-start(bf16[32,1,256,512]{3,2,1,0:T(8,128)(2,1)} %stack.24), calls=%async_computation.2 | async-start | bytes 16777216 | tf_op jit(solution)/shard_map/all_to_all | solution.py:63
  299.7 0.6 iota_compare_fusion.4
  300.3 179.8 %all-to-all-done.2 = bf16[32,1,256,512]{3,2,1,0:T(8,128)(2,1)} async-done(((bf16[32,1,256,512]{3,2,1,0:T(8,128)(2,1)}), bf16[32,1,256,512]{3,2,1,0:T(8,128)(2,1)}, u32[]{:S(2)}, u32[]{:S(2)}) %all-to-all-start.2) | async-done | bytes 8388640 | tf_op jit(solution)/shard_map/all_to_all | solution.py:63
  480.1 6.1 gather_fusion.1
  486.3 7.6 fusion.12
  493.9 10.5 %copy.49 = f32[16,256,512]{2,0,1:T(8,128)} copy(f32[16,256,512]{1,2,0:T(8,128)} %fusion.12) | data formatting | bytes 16777216 | tf_op jit(solution)/shard_map/tij,tjw->tiw/dot_general | solution.py:31
  504.3 10.9 %convolution_add_fusion = f32[12,256,512]{2,0,1:T(8,128)S(1)} fusion(f32[12,256,512]{2,0,1:T(8,128)} %copy-done.1, f32[16,256,512]{2,0,1:T(8,128)} %copy.49, s32[16]{0:T(128)S(1)} %get-tuple-element.21, pred[16]{0:T(512)(128)(4,1)S(1)} %iota_compare_fusion.4), kind=kOutput, calls=%fused_computation.12 | convolution fusion | flops 303563136 | bytes 20971600 | tf_op jit(solution)/shard_map/tk,tiw->kiw/dot_general | solution.py:35
  515.2 3.2 copy-done.2
  518.4 0.6 slice_bitcast_fusion
  519.0 0.7 copy.50
  519.7 25.1 %all_to_all.36 = f32[4,1,256,512]{3,2,1,0:T(8,128)S(1)} all-to-all(f32[4,1,256,512]{3,2,1,0:T(8,128)S(1)} %copy.50), channel_id=1, replica_groups=mesh['grp'=2,'row'=4,'col'=32] {'row'}, dimensions={0} | all-to-all | bytes 4194304 | tf_op jit(solution)/shard_map/all_to_all | solution.py:15
  544.8 1.0 reduce_sum.39
  545.8 2.8 bitcast_convert_fusion
  548.5 4.2 stack.27
  552.7 14.4 %all-to-all-start.4 = ((bf16[32,1,256,512]{3,2,1,0:T(8,128)(2,1)}), bf16[32,1,256,512]{3,2,1,0:T(8,128)(2,1)}, u32[]{:S(2)}, u32[]{:S(2)}) async-start(bf16[32,1,256,512]{3,2,1,0:T(8,128)(2,1)} %stack.27), calls=%async_computation.4 | async-start | bytes 16777216 | tf_op jit(solution)/shard_map/all_to_all | solution.py:63
  567.2 0.7 iota_compare_fusion.3
  567.8 179.7 %all-to-all-done.4 = bf16[32,1,256,512]{3,2,1,0:T(8,128)(2,1)} async-done(((bf16[32,1,256,512]{3,2,1,0:T(8,128)(2,1)}), bf16[32,1,256,512]{3,2,1,0:T(8,128)(2,1)}, u32[]{:S(2)}, u32[]{:S(2)}) %all-to-all-start.4) | async-done | bytes 8388640 | tf_op jit(solution)/shard_map/all_to_all | solution.py:63
  747.6 6.1 gather_fusion.2
  753.7 7.6 fusion.15
  761.3 10.5 %copy.53 = f32[16,256,512]{2,0,1:T(8,128)} copy(f32[16,256,512]{1,2,0:T(8,128)} %fusion.15) | data formatting | bytes 16777216 | tf_op jit(solution)/shard_map/tij,tjw->tiw/dot_general | solution.py:31
  771.8 12.8 %fusion.54 = f32[12,256,512]{2,0,1:T(8,128)S(1)} fusion(f32[16,256,512]{2,0,1:T(8,128)} %copy.53, s32[16]{0:T(128)S(1)} %get-tuple-element.19, pred[16]{0:T(512)(128)(4,1)S(1)} %iota_compare_fusion.3), kind=kOutput, calls=%fused_computation.63 | convolution fusion | flops 301990272 | bytes 14680144 | tf_op jit(solution)/shard_map/tk,tiw->kiw/dot_general | solution.py:35
  784.6 3.2 fusion.18
  787.8 2.0 copy.54
  789.7 3.6 all-to-all-start.5
  793.4 2.3 maximum_bitcast_fusion
  795.7 20.4 %all-to-all-done.5 = f32[4,1,256,512]{3,2,1,0:T(8,128)S(1)} async-done(((f32[4,1,256,512]{3,2,1,0:T(8,128)}), f32[4,1,256,512]{3,2,1,0:T(8,128)S(1)}, u32[]{:S(2)}, u32[]{:S(2)}) %all-to-all-start.5) | async-done | bytes 2097184 | tf_op jit(solution)/shard_map/all_to_all | solution.py:15
  816.1 0.2 reduce_sum.40
  816.3 0.1 broadcast_in_dim.25
  816.4 8.7 %all_to_all.37 = f32[2,256,512]{2,1,0:T(8,128)S(1)} all-to-all(f32[2,256,512]{2,1,0:T(8,128)S(1)} %broadcast_in_dim.25), channel_id=1, replica_groups=mesh['grp'=2,'row'=4,'col'=32] {'grp'}, dimensions={0} | all-to-all | bytes 2097152 | tf_op jit(solution)/shard_map/all_to_all | solution.py:21
  825.3 1.0 convolution_bitcast_fusion
  826.3 1.0 copy.56
  (18 shorter events, 0.2 us)
Async XLA Ops:
  0.6 824.7 %copy-start = (f32[1,1,256,256]{3,2,1,0:T(8,128)S(1)}, f32[1,1,256,256]{3,2,1,0:T(8,128)}, u32[]{:S(2)}) copy-start(f32[1,1,256,256]{3,2,1,0:T(8,128)} %param.13) | copy-start | bytes 786436
  6.6 12.1 %copy-start.4 = (s32[1,1,1,3]{3,2,1,0:T(1,128)S(1)}, s32[1,1,1,3]{3,2,1,0:T(1,128)}, u32[]{:S(2)}) copy-start(s32[1,1,1,3]{3,2,1,0:T(1,128)} %param.17) | copy-start | bytes 40
  6.6 13.4 %copy-start.6 = (s32[1,1,1,3,16]{4,2,3,1,0:T(1,128)S(1)}, s32[1,1,1,3,16]{4,2,3,1,0:T(1,128)}, u32[]{:S(2)}) copy-start(s32[1,1,1,3,16]{4,2,3,1,0:T(1,128)} %param.16) | copy-start | bytes 580
  6.6 13.5 %copy-start.5 = (s32[1,1,1,3,16]{4,2,3,1,0:T(1,128)S(1)}, s32[1,1,1,3,16]{4,2,3,1,0:T(1,128)}, u32[]{:S(2)}) copy-start(s32[1,1,1,3,16]{4,2,3,1,0:T(1,128)} %param.15) | copy-start | bytes 580
  6.6 199.7 %all-to-all-start = ((bf16[32,1,256,512]{3,2,1,0:T(8,128)(2,1)}), bf16[32,1,256,512]{3,2,1,0:T(8,128)(2,1)}, u32[]{:S(2)}, u32[]{:S(2)}) async-start(bf16[32,1,256,512]{3,2,1,0:T(8,128)(2,1)} %stack.22), calls=%async_computation | async-start | bytes 16777216 | tf_op jit(solution)/shard_map/all_to_all | solution.py:63
  243.3 3.2 copy-start.1
  282.9 197.3 %all-to-all-start.2 = ((bf16[32,1,256,512]{3,2,1,0:T(8,128)(2,1)}), bf16[32,1,256,512]{3,2,1,0:T(8,128)(2,1)}, u32[]{:S(2)}, u32[]{:S(2)}) async-start(bf16[32,1,256,512]{3,2,1,0:T(8,128)(2,1)} %stack.24), calls=%async_computation.2 | async-start | bytes 16777216 | tf_op jit(solution)/shard_map/all_to_all | solution.py:63
  515.2 3.2 copy-start.2
  552.7 194.9 %all-to-all-start.4 = ((bf16[32,1,256,512]{3,2,1,0:T(8,128)(2,1)}), bf16[32,1,256,512]{3,2,1,0:T(8,128)(2,1)}, u32[]{:S(2)}, u32[]{:S(2)}) async-start(bf16[32,1,256,512]{3,2,1,0:T(8,128)(2,1)} %stack.27), calls=%async_computation.4 | async-start | bytes 16777216 | tf_op jit(solution)/shard_map/all_to_all | solution.py:63
  789.7 26.3 %all-to-all-start.5 = ((f32[4,1,256,512]{3,2,1,0:T(8,128)}), f32[4,1,256,512]{3,2,1,0:T(8,128)S(1)}, u32[]{:S(2)}, u32[]{:S(2)}) async-start(f32[4,1,256,512]{3,2,1,0:T(8,128)} %copy.54), calls=%async_computation.5 | async-start | bytes 4194304 | tf_op jit(solution)/shard_map/all_to_all | solution.py:15
  795.7 29.6 %copy-start.3 = (f32[1,1,256,512]{3,2,1,0:T(8,128)S(1)}, f32[1,1,256,512]{3,2,1,0:T(8,128)}, u32[]{:S(2)}) copy-start(f32[1,1,256,512]{3,2,1,0:T(8,128)} %param.12) | copy-start | bytes 1572868
